TPU v7x, 32 devices: a whole 2x2x4 slice. The times are simulated.
32 devices in a mesh: gx: 8 (over y, x, core), gy: 4 (over z).
Axes of the slice: x: 2, y: 2, z: 4, core: 2. Of those that a mesh axis runs over, the one named last changes fastest.
Arguments:
- tiles: float32 [256, 5, 128, 128], P(('gx', 'gy')), may hold values from 0 to 0.003125
- cols: int32 [256, 5], P(('gx', 'gy')), may hold values from 0 to 17, as said below
- boundary: int32 [32, 2], P(('gx', 'gy')), may hold values from 0 to 7, as said below
- current: float32 [32768, 64], P(('gx', 'gy')), may hold values from -44 to 44
- previous: float32 [32768, 64], P(('gx', 'gy')), may hold values from -44 to 44
Outputs:
- filtered: float32 [32768, 64], P(('gx', 'gy'))
- gram: float32 [64, 64], replicated
Inputs may be any that keep to these rules, and one draw needn't show every extreme that they name: `cols`: in each part, block row r has r in its first tile slot; each value from 8 up to the table's last entry occurs exactly once among the part's block rows. `boundary`: the 2 entries of a row are distinct block rows of the part.
All inputs are finite; a program needn't handle non-finite values.
Results may differ from a plain program's by a relative error of at most 0.0003.
Values sent between devices are 32-bit elements; how exact they have to be, the bound alone decides.
A program may use at most 64 MiB of HBM per device.

v0:
```python
import jax
import jax.numpy as jnp
from jax import lax
from jax.sharding import PartitionSpec as P

ITERS = 3


def partner(value, axis, stride):
    mask = 2**stride
    pairs = [(source, source ^ mask) for source in range(lax.axis_size(axis))]
    return lax.ppermute(value, axis, pairs)


def shards(tiles, cols, boundary, current, previous):
    size_x = lax.axis_size("gx")
    size_y = lax.axis_size("gy")
    block_rows = cols.shape[0]
    block_size = tiles.shape[-1]
    vectors = current.shape[1]
    bits_low = list(range(size_y.bit_length() - 1))
    bits_high = list(range(size_x.bit_length() - 1))
    field = current
    older = previous
    for step in range(ITERS):
        blocks = field.reshape(block_rows, block_size, vectors)
        outgoing = jnp.take(blocks, boundary[0], axis=0)

        def from_low():
            return [partner(outgoing, "gy", which_bit) for which_bit in bits_low]

        def from_high():
            return [partner(outgoing, "gx", which_bit) for which_bit in bits_high]

        low_ghosts = from_low()
        high_ghosts = from_high()
        table = jnp.concatenate([blocks] + low_ghosts + high_ghosts, axis=0)
        operands = jnp.take(table, cols, axis=0)
        product = jnp.einsum("rtij,rtjv->riv", tiles, operands, precision=lax.Precision.HIGHEST)
        product = product.reshape(block_rows * block_size, vectors)
        nexter = 2.0 / 0.75 * (product - 0.25 * field) - older
        older = field
        field = nexter
    partial_gram = jnp.dot(
        field.T, field, precision=lax.Precision.HIGHEST, preferred_element_type=jnp.float32
    )
    total_rows = block_rows * block_size * size_x * size_y
    gram = lax.psum(partial_gram, ("gx", "gy")) / float(total_rows)
    return (field, gram)


def solution(mesh):
    in_specs = (
        P(("gx", "gy"), None, None, None),
        P(("gx", "gy"), None),
        P(("gx", "gy"), None),
        P(("gx", "gy"), None),
        P(("gx", "gy"), None),
    )
    out_specs = (P(("gx", "gy"), None), P())
    return jax.shard_map(shards, mesh=mesh, in_specs=in_specs, out_specs=out_specs, check_vma=False)
```

profile of v0, /device:TPU:0, one launch (start us, length us, event | category | flops | bytes accessed | tf_op | source)
XLA Modules:
  0.0 96.7 jit_solution(13172485153724881354)
XLA Ops:
  0.6 0.8 compare_and_fusion.1
  1.5 0.7 compare_select_fusion.1
  2.1 1.0 copy_bitcast_fusion.2
  3.7 3.0 %collective-permute-start.4 = (f32[2,128,64]{1,2,0:T(8,128)S(1)}, f32[2,128,64]{1,2,0:T(8,128)S(1)}, u32[]{:S(2)}, u32[]{:S(2)}) collective-permute-start(f32[2,128,64]{1,2,0:T(8,128)S(1)} %broadcast_select_fusion.2), channel_id=1, source_target_pairs={{0,16},{4,20},{8,24},{12,28},{16,0},{20,4},{24,8},{28,12},{1,17},{... | collective-permute-start | bytes 196616 | tf_op jit(solution)/shard_map/ppermute | solution.py:12
  6.7 1.5 %collective-permute-start.3 = (f32[2,128,64]{1,2,0:T(8,128)S(1)}, f32[2,128,64]{1,2,0:T(8,128)S(1)}, u32[]{:S(2)}, u32[]{:S(2)}) collective-permute-start(f32[2,128,64]{1,2,0:T(8,128)S(1)} %broadcast_select_fusion.2), channel_id=1, source_target_pairs={{0,8},{4,12},{8,0},{12,4},{16,24},{20,28},{24,16},{28,20},{1,9},{5... | collective-permute-start | bytes 196616 | tf_op jit(solution)/shard_map/ppermute | solution.py:12
  8.2 2.6 %collective-permute-start.1 = (f32[2,128,64]{1,2,0:T(8,128)S(1)}, f32[2,128,64]{1,2,0:T(8,128)S(1)}, u32[]{:S(2)}, u32[]{:S(2)}) collective-permute-start(f32[2,128,64]{1,2,0:T(8,128)S(1)} %broadcast_select_fusion.2), channel_id=1, source_target_pairs={{0,2},{1,3},{2,0},{3,1},{4,6},{5,7},{6,4},{7,5},{8,10},{9,11},{10,... | collective-permute-start | bytes 196616 | tf_op jit(solution)/shard_map/ppermute | solution.py:12
  10.8 1.6 %collective-permute-start = (f32[2,128,64]{1,2,0:T(8,128)S(1)}, f32[2,128,64]{1,2,0:T(8,128)}, u32[]{:S(2)}, u32[]{:S(2)}) collective-permute-start(f32[2,128,64]{1,2,0:T(8,128)S(1)} %broadcast_select_fusion.2), channel_id=1, source_target_pairs={{0,1},{1,0},{2,3},{3,2},{4,5},{5,4},{6,7},{7,6},{8,9},{9,8},{10,11... | collective-permute-start | bytes 196616 | tf_op jit(solution)/shard_map/ppermute | solution.py:12
  12.4 0.7 compare_and_fusion
  13.1 0.7 compare_select_fusion
  13.8 1.0 constant_dynamic-update-slice_fusion.5
  15.3 0.7 pad_clamp_fusion
  16.0 0.8 constant_dynamic-update-slice_fusion.4
  16.9 1.7 %gather_fusion.1 = f32[40,128,64]{1,2,0:T(8,128)} fusion(f32[18,128,64]{1,2,0:T(8,128)S(1)} %constant_dynamic-update-slice_fusion, s32[1024]{0:T(1024)S(1)} %pad_clamp_fusion), kind=kCustom, calls=%fused_computation.1.clone | custom fusion | bytes 2621600 | tf_op jit(solution)/shard_map/jit(_take)/gather | solution.py:38
  18.6 4.7 %fusion.6 = f32[8,8,8,128]{3,2,1,0:T(8,128)S(1)} fusion(f32[8,5,128,128]{3,2,1,0:T(8,128)S(1)} %copy-done, f32[8,5,128,64]{2,3,1,0:T(8,128)} %bitcast.85, pred[8,5]{1,0:T(8,128)(4,1)S(1)} %compare_and_fusion), kind=kOutput, calls=%fused_computation.12 | convolution fusion | flops 503644160 | bytes 4194344 | tf_op jit(solution)/shard_map/rtij,rtjv->riv/dot_general | solution.py:39
  23.4 0.7 copy-done.2
  25.8 0.8 collective-permute-start.6
  26.6 1.5 %collective-permute-start.5 = (f32[2,128,64]{1,2,0:T(8,128)S(1)}, f32[2,128,64]{1,2,0:T(8,128)S(1)}, u32[]{:S(2)}, u32[]{:S(2)}) collective-permute-start(f32[2,128,64]{1,2,0:T(8,128)S(1)} %broadcast_select_fusion.1), channel_id=1, source_target_pairs={{0,1},{1,0},{2,3},{3,2},{4,5},{5,4},{6,7},{7,6},{8,9},{9,8},{10,11... | collective-permute-start | bytes 196616 | tf_op jit(solution)/shard_map/ppermute | solution.py:12
  28.1 1.1 %constant_dynamic-update-slice_fusion.11 = f32[18,128,64]{1,2,0:T(8,128)S(1)} fusion(f32[1024,64]{0,1:T(8,128)} %param.13, f32[1024,64]{0,1:T(8,128)S(1)} %copy-done.1, f32[8,8,8,128]{3,2,1,0:T(8,128)} %copy-done.2), kind=kLoop, calls=%fused_computation.45 | loop fusion | flops 262143 | bytes 1048576
  29.1 2.0 %collective-permute-done.5 = f32[2,128,64]{1,2,0:T(8,128)S(1)} collective-permute-done((f32[2,128,64]{1,2,0:T(8,128)S(1)}, f32[2,128,64]{1,2,0:T(8,128)S(1)}, u32[]{:S(2)}, u32[]{:S(2)}) %collective-permute-start.5) | collective-permute-done | bytes 65568 | tf_op jit(solution)/shard_map/ppermute | solution.py:12
  31.2 1.4 %collective-permute-done.6 = f32[2,128,64]{1,2,0:T(8,128)S(1)} collective-permute-done((f32[2,128,64]{1,2,0:T(8,128)S(1)}, f32[2,128,64]{1,2,0:T(8,128)S(1)}, u32[]{:S(2)}, u32[]{:S(2)}) %collective-permute-start.6) | collective-permute-done | bytes 65568 | tf_op jit(solution)/shard_map/ppermute | solution.py:12
  32.7 1.7 %gather_fusion.3 = f32[40,128,64]{1,2,0:T(8,128)} fusion(f32[18,128,64]{1,2,0:T(8,128)S(1)} %constant_dynamic-update-slice_fusion.6, s32[1024]{0:T(1024)S(1)} %pad_clamp_fusion), kind=kCustom, calls=%fused_computation.4.clone | custom fusion | bytes 2621600 | tf_op jit(solution)/shard_map/jit(_take)/gather | solution.py:38
  34.4 4.8 %fusion.9 = f32[8,8,8,128]{3,2,1,0:T(8,128)S(1)} fusion(f32[8,5,128,128]{3,2,1,0:T(8,128)S(1)} %copy-done, f32[8,5,128,64]{2,3,1,0:T(8,128)} %bitcast.86, pred[8,5]{1,0:T(8,128)(4,1)S(1)} %compare_and_fusion), kind=kOutput, calls=%fused_computation.13 | convolution fusion | flops 503644160 | bytes 4194344 | tf_op jit(solution)/shard_map/rtij,rtjv->riv/dot_general | solution.py:39
  39.9 0.7 copy-done.10
  41.2 1.5 %collective-permute-start.14 = (f32[2,128,64]{1,2,0:T(8,128)S(1)}, f32[2,128,64]{1,2,0:T(8,128)S(1)}, u32[]{:S(2)}, u32[]{:S(2)}) collective-permute-start(f32[2,128,64]{1,2,0:T(8,128)S(1)} %broadcast_select_fusion), channel_id=1, source_target_pairs={{0,16},{4,20},{8,24},{12,28},{16,0},{20,4},{24,8},{28,12},{1,17},{... | collective-permute-start | bytes 196616 | tf_op jit(solution)/shard_map/ppermute | solution.py:12
  42.8 1.5 %collective-permute-start.13 = (f32[2,128,64]{1,2,0:T(8,128)S(1)}, f32[2,128,64]{1,2,0:T(8,128)S(1)}, u32[]{:S(2)}, u32[]{:S(2)}) collective-permute-start(f32[2,128,64]{1,2,0:T(8,128)S(1)} %broadcast_select_fusion), channel_id=1, source_target_pairs={{0,8},{4,12},{8,0},{12,4},{16,24},{20,28},{24,16},{28,20},{1,9},{5... | collective-permute-start | bytes 196616 | tf_op jit(solution)/shard_map/ppermute | solution.py:12
  44.3 0.9 collective-permute-start.11
  45.2 1.7 %collective-permute-start.10 = (f32[2,128,64]{1,2,0:T(8,128)S(1)}, f32[2,128,64]{1,2,0:T(8,128)S(1)}, u32[]{:S(2)}, u32[]{:S(2)}) collective-permute-start(f32[2,128,64]{1,2,0:T(8,128)S(1)} %broadcast_select_fusion), channel_id=1, source_target_pairs={{0,1},{1,0},{2,3},{3,2},{4,5},{5,4},{6,7},{7,6},{8,9},{9,8},{10,11... | collective-permute-start | bytes 196616 | tf_op jit(solution)/shard_map/ppermute | solution.py:12
  46.8 1.0 constant_dynamic-update-slice_fusion.17
  47.8 3.0 %collective-permute-done.10 = f32[2,128,64]{1,2,0:T(8,128)S(1)} collective-permute-done((f32[2,128,64]{1,2,0:T(8,128)S(1)}, f32[2,128,64]{1,2,0:T(8,128)S(1)}, u32[]{:S(2)}, u32[]{:S(2)}) %collective-permute-start.10) | collective-permute-done | bytes 65568 | tf_op jit(solution)/shard_map/ppermute | solution.py:12
  50.9 1.7 %gather_fusion.5 = f32[40,128,64]{1,2,0:T(8,128)} fusion(f32[18,128,64]{1,2,0:T(8,128)S(1)} %constant_dynamic-update-slice_fusion.12, s32[1024]{0:T(1024)S(1)} %pad_clamp_fusion), kind=kCustom, calls=%fused_computation.5.clone | custom fusion | bytes 2621600 | tf_op jit(solution)/shard_map/jit(_take)/gather | solution.py:38
  52.6 4.8 %fusion.12 = f32[8,8,8,128]{3,2,1,0:T(8,128)S(1)} fusion(f32[8,5,128,128]{3,2,1,0:T(8,128)S(1)} %copy-done, f32[8,5,128,64]{2,3,1,0:T(8,128)} %bitcast.84, pred[8,5]{1,0:T(8,128)(4,1)S(1)} %compare_and_fusion), kind=kOutput, calls=%fused_computation.14 | convolution fusion | flops 503644160 | bytes 4194344 | tf_op jit(solution)/shard_map/rtij,rtjv->riv/dot_general | solution.py:39
  57.9 38.2 %psum.7 = f32[64,64]{1,0:T(8,128)S(1)} all-reduce(f32[64,64]{1,0:T(8,128)S(1)} %fusion.32), channel_id=1, replica_groups=mesh['gx'=8,'gy'=4] {'gx','gy'}, use_global_device_ids=true, to_apply=%region_0.3 | all-reduce | flops 4096 | bytes 32768 | tf_op jit(solution)/shard_map/psum | solution.py:48
  (67 shorter events, 5.6 us)
Async XLA Ops:
  0.6 18.0 %copy-start = (f32[8,5,128,128]{3,2,1,0:T(8,128)S(1)}, f32[8,5,128,128]{3,2,1,0:T(8,128)}, u32[]{:S(2)}) copy-start(f32[8,5,128,128]{3,2,1,0:T(8,128)} %param.9) | copy-start | bytes 7864324
  3.7 13.2 %collective-permute-start.4 = (f32[2,128,64]{1,2,0:T(8,128)S(1)}, f32[2,128,64]{1,2,0:T(8,128)S(1)}, u32[]{:S(2)}, u32[]{:S(2)}) collective-permute-start(f32[2,128,64]{1,2,0:T(8,128)S(1)} %broadcast_select_fusion.2), channel_id=1, source_target_pairs={{0,16},{4,20},{8,24},{12,28},{16,0},{20,4},{24,8},{28,12},{1,17},{... | collective-permute-start | bytes 196616 | tf_op jit(solution)/shard_map/ppermute | solution.py:12
  6.7 10.2 %collective-permute-start.3 = (f32[2,128,64]{1,2,0:T(8,128)S(1)}, f32[2,128,64]{1,2,0:T(8,128)S(1)}, u32[]{:S(2)}, u32[]{:S(2)}) collective-permute-start(f32[2,128,64]{1,2,0:T(8,128)S(1)} %broadcast_select_fusion.2), channel_id=1, source_target_pairs={{0,8},{4,12},{8,0},{12,4},{16,24},{20,28},{24,16},{28,20},{1,9},{5... | collective-permute-start | bytes 196616 | tf_op jit(solution)/shard_map/ppermute | solution.py:12
  8.2 8.6 %collective-permute-start.2 = (f32[2,128,64]{1,2,0:T(8,128)S(1)}, f32[2,128,64]{1,2,0:T(8,128)S(1)}, u32[]{:S(2)}, u32[]{:S(2)}) collective-permute-start(f32[2,128,64]{1,2,0:T(8,128)S(1)} %broadcast_select_fusion.2), channel_id=1, source_target_pairs={{0,4},{4,0},{8,12},{12,8},{16,20},{20,16},{24,28},{28,24},{1,5},{5... | collective-permute-start | bytes 196616 | tf_op jit(solution)/shard_map/ppermute | solution.py:12
  8.2 8.6 %collective-permute-start.1 = (f32[2,128,64]{1,2,0:T(8,128)S(1)}, f32[2,128,64]{1,2,0:T(8,128)S(1)}, u32[]{:S(2)}, u32[]{:S(2)}) collective-permute-start(f32[2,128,64]{1,2,0:T(8,128)S(1)} %broadcast_select_fusion.2), channel_id=1, source_target_pairs={{0,2},{1,3},{2,0},{3,1},{4,6},{5,7},{6,4},{7,5},{8,10},{9,11},{10,... | collective-permute-start | bytes 196616 | tf_op jit(solution)/shard_map/ppermute | solution.py:12
  10.8 5.2 %collective-permute-start = (f32[2,128,64]{1,2,0:T(8,128)S(1)}, f32[2,128,64]{1,2,0:T(8,128)}, u32[]{:S(2)}, u32[]{:S(2)}) collective-permute-start(f32[2,128,64]{1,2,0:T(8,128)S(1)} %broadcast_select_fusion.2), channel_id=1, source_target_pairs={{0,1},{1,0},{2,3},{3,2},{4,5},{5,4},{6,7},{7,6},{8,9},{9,8},{10,11... | collective-permute-start | bytes 196616 | tf_op jit(solution)/shard_map/ppermute | solution.py:12
  18.6 5.5 %copy-start.1 = (f32[1024,64]{0,1:T(8,128)S(1)}, f32[1024,64]{0,1:T(8,128)}, u32[]{:S(2)}) copy-start(f32[1024,64]{0,1:T(8,128)} %param.12) | copy-start | bytes 786436
  18.6 5.5 %copy-start.5 = (f32[1024,64]{0,1:T(8,128)S(1)}, f32[1024,64]{0,1:T(8,128)}, u32[]{:S(2)}) copy-start(f32[1024,64]{0,1:T(8,128)} %param.13) | copy-start | bytes 786436
  23.4 0.7 copy-start.2
  24.8 7.9 %collective-permute-start.9 = (f32[2,128,64]{1,2,0:T(8,128)S(1)}, f32[2,128,64]{1,2,0:T(8,128)S(1)}, u32[]{:S(2)}, u32[]{:S(2)}) collective-permute-start(f32[2,128,64]{1,2,0:T(8,128)S(1)} %broadcast_select_fusion.1), channel_id=1, source_target_pairs={{0,16},{4,20},{8,24},{12,28},{16,0},{20,4},{24,8},{28,12},{1,17},{... | collective-permute-start | bytes 196616 | tf_op jit(solution)/shard_map/ppermute | solution.py:12
  25.3 7.4 %collective-permute-start.8 = (f32[2,128,64]{1,2,0:T(8,128)S(1)}, f32[2,128,64]{1,2,0:T(8,128)S(1)}, u32[]{:S(2)}, u32[]{:S(2)}) collective-permute-start(f32[2,128,64]{1,2,0:T(8,128)S(1)} %broadcast_select_fusion.1), channel_id=1, source_target_pairs={{0,8},{4,12},{8,0},{12,4},{16,24},{20,28},{24,16},{28,20},{1,9},{5... | collective-permute-start | bytes 196616 | tf_op jit(solution)/shard_map/ppermute | solution.py:12
  25.8 6.8 %collective-permute-start.7 = (f32[2,128,64]{1,2,0:T(8,128)S(1)}, f32[2,128,64]{1,2,0:T(8,128)S(1)}, u32[]{:S(2)}, u32[]{:S(2)}) collective-permute-start(f32[2,128,64]{1,2,0:T(8,128)S(1)} %broadcast_select_fusion.1), channel_id=1, source_target_pairs={{0,4},{4,0},{8,12},{12,8},{16,20},{20,16},{24,28},{28,24},{1,5},{5... | collective-permute-start | bytes 196616 | tf_op jit(solution)/shard_map/ppermute | solution.py:12
  25.8 6.8 %collective-permute-start.6 = (f32[2,128,64]{1,2,0:T(8,128)S(1)}, f32[2,128,64]{1,2,0:T(8,128)S(1)}, u32[]{:S(2)}, u32[]{:S(2)}) collective-permute-start(f32[2,128,64]{1,2,0:T(8,128)S(1)} %broadcast_select_fusion.1), channel_id=1, source_target_pairs={{0,2},{1,3},{2,0},{3,1},{4,6},{5,7},{6,4},{7,5},{8,10},{9,11},{10,... | collective-permute-start | bytes 196616 | tf_op jit(solution)/shard_map/ppermute | solution.py:12
  26.6 4.6 %collective-permute-start.5 = (f32[2,128,64]{1,2,0:T(8,128)S(1)}, f32[2,128,64]{1,2,0:T(8,128)S(1)}, u32[]{:S(2)}, u32[]{:S(2)}) collective-permute-start(f32[2,128,64]{1,2,0:T(8,128)S(1)} %broadcast_select_fusion.1), channel_id=1, source_target_pairs={{0,1},{1,0},{2,3},{3,2},{4,5},{5,4},{6,7},{7,6},{8,9},{9,8},{10,11... | collective-permute-start | bytes 196616 | tf_op jit(solution)/shard_map/ppermute | solution.py:12
  34.4 4.8 %copy-start.3 = (f32[8,8,8,128]{3,2,1,0:T(8,128)S(1)}, f32[8,8,8,128]{3,2,1,0:T(8,128)}, u32[]{:S(2)}) copy-start(f32[8,8,8,128]{3,2,1,0:T(8,128)} %copy-done.2) | copy-start | bytes 786436
  34.4 4.8 %copy-start.6 = (f32[1024,64]{0,1:T(8,128)S(1)}, f32[1024,64]{0,1:T(8,128)}, u32[]{:S(2)}) copy-start(f32[1024,64]{0,1:T(8,128)} %param.13) | copy-start | bytes 786436
  39.2 0.7 copy-start.8
  39.9 0.7 copy-start.10
  41.2 9.6 %collective-permute-start.14 = (f32[2,128,64]{1,2,0:T(8,128)S(1)}, f32[2,128,64]{1,2,0:T(8,128)S(1)}, u32[]{:S(2)}, u32[]{:S(2)}) collective-permute-start(f32[2,128,64]{1,2,0:T(8,128)S(1)} %broadcast_select_fusion), channel_id=1, source_target_pairs={{0,16},{4,20},{8,24},{12,28},{16,0},{20,4},{24,8},{28,12},{1,17},{... | collective-permute-start | bytes 196616 | tf_op jit(solution)/shard_map/ppermute | solution.py:12
  42.8 8.1 %collective-permute-start.13 = (f32[2,128,64]{1,2,0:T(8,128)S(1)}, f32[2,128,64]{1,2,0:T(8,128)S(1)}, u32[]{:S(2)}, u32[]{:S(2)}) collective-permute-start(f32[2,128,64]{1,2,0:T(8,128)S(1)} %broadcast_select_fusion), channel_id=1, source_target_pairs={{0,8},{4,12},{8,0},{12,4},{16,24},{20,28},{24,16},{28,20},{1,9},{5... | collective-permute-start | bytes 196616 | tf_op jit(solution)/shard_map/ppermute | solution.py:12
  44.3 6.6 %collective-permute-start.12 = (f32[2,128,64]{1,2,0:T(8,128)S(1)}, f32[2,128,64]{1,2,0:T(8,128)S(1)}, u32[]{:S(2)}, u32[]{:S(2)}) collective-permute-start(f32[2,128,64]{1,2,0:T(8,128)S(1)} %broadcast_select_fusion), channel_id=1, source_target_pairs={{0,4},{4,0},{8,12},{12,8},{16,20},{20,16},{24,28},{28,24},{1,5},{5... | collective-permute-start | bytes 196616 | tf_op jit(solution)/shard_map/ppermute | solution.py:12
  44.3 6.5 %collective-permute-start.11 = (f32[2,128,64]{1,2,0:T(8,128)S(1)}, f32[2,128,64]{1,2,0:T(8,128)S(1)}, u32[]{:S(2)}, u32[]{:S(2)}) collective-permute-start(f32[2,128,64]{1,2,0:T(8,128)S(1)} %broadcast_select_fusion), channel_id=1, source_target_pairs={{0,2},{1,3},{2,0},{3,1},{4,6},{5,7},{6,4},{7,5},{8,10},{9,11},{10,... | collective-permute-start | bytes 196616 | tf_op jit(solution)/shard_map/ppermute | solution.py:12
  45.2 5.6 %collective-permute-start.10 = (f32[2,128,64]{1,2,0:T(8,128)S(1)}, f32[2,128,64]{1,2,0:T(8,128)S(1)}, u32[]{:S(2)}, u32[]{:S(2)}) collective-permute-start(f32[2,128,64]{1,2,0:T(8,128)S(1)} %broadcast_select_fusion), channel_id=1, source_target_pairs={{0,1},{1,0},{2,3},{3,2},{4,5},{5,4},{6,7},{7,6},{8,9},{9,8},{10,11... | collective-permute-start | bytes 196616 | tf_op jit(solution)/shard_map/ppermute | solution.py:12
  52.6 4.8 %copy-start.4 = (f32[8,8,8,128]{3,2,1,0:T(8,128)S(1)}, f32[8,8,8,128]{3,2,1,0:T(8,128)}, u32[]{:S(2)}) copy-start(f32[8,8,8,128]{3,2,1,0:T(8,128)} %copy-done.2) | copy-start | bytes 786436
  52.6 4.8 %copy-start.7 = (f32[1024,64]{0,1:T(8,128)S(1)}, f32[1024,64]{0,1:T(8,128)}, u32[]{:S(2)}) copy-start(f32[1024,64]{0,1:T(8,128)} %param.13) | copy-start | bytes 786436
  52.6 4.8 %copy-start.9 = (f32[8,8,8,128]{3,2,1,0:T(8,128)S(1)}, f32[8,8,8,128]{3,2,1,0:T(8,128)}, u32[]{:S(2)}) copy-start(f32[8,8,8,128]{3,2,1,0:T(8,128)} %copy-done.8) | copy-start | bytes 786436
  57.5 39.2 %copy-start.11 = (f32[1024,64]{0,1:T(8,128)}, f32[1024,64]{0,1:T(8,128)S(1)}, u32[]{:S(2)}) copy-start(f32[1024,64]{0,1:T(8,128)S(1)} %fusion.22) | copy-start | bytes 786436
where the time goes:
time: 97.2 us; the launch traced here: 96.7 us
  blocking collectives  38.2 us (39%)
  starting transfers between devices  17.5 us (18%)
  matrix products  14.6 us (15%)
  local copies, waits for them, and re-layouts  13.2 us (14%)
  waiting for transfers between devices  6.51 us (7%)
  other arithmetic  5.71 us (6%)
    psum x1, blocking collectives, shards(): gram = lax.psum(partial_gram, ('gx', 'gy')) / float(total_rows)  38.2 us
    ppermute x15, starting transfers between devices, partner(): return lax.ppermute(value, axis, pairs)  17.5 us
    dot_general x3, matrix products, shards(): jnp.einsum('rtij,rtjv->riv', tiles, operands, precision=lax.Precision.HIG...  14.3 us
    ppermute x15, waiting for transfers between devices, partner(): return lax.ppermute(value, axis, pairs)  6.51 us
    gather x3, local copies, waits for them, and re-layouts, shards(): operands = jnp.take(table, cols, axis=0)  5.09 us
    unnamed x38, local copies, waits for them, and re-layouts  4.88 us
  transfers between devices with their start and end apart: 15, of which 3 were waited for; matrix products, arithmetic and copies ran while one was open for 7% of the time, Pallas kernels for 0%

commit v1 on v0

--- a/solution.py
+++ b/solution.py
@@ -45,7 +45,7 @@
         field.T, field, precision=lax.Precision.HIGHEST, preferred_element_type=jnp.float32
     )
     total_rows = block_rows * block_size * size_x * size_y
-    gram = lax.psum(partial_gram, ("gx", "gy")) / float(total_rows)
+    gram = jnp.sum(lax.all_gather(partial_gram, ("gx", "gy")), axis=0) / float(total_rows)
     return (field, gram)
 
 

time: 97.2 us -> 140 us (1.44)
  blocking collectives: 38.2 us -> 79.6 us
    all_gather x0 -> x1, blocking collectives: none -> 79.6 us  [shards(): lax.all_gather(partial_gram, ('gx', 'gy'))]
    psum x1 -> x0, blocking collectives: 38.2 us -> none  [shards(): gram = lax.psum(partial_gram, ('gx', 'gy')) / float(total_rows)]
  transfers between devices with their start and end apart: 15 -> 15, of which waited for: 3 -> 3; matrix products, arithmetic and copies ran while one was open for 7% -> 5% of each run, Pallas kernels for 0% -> 0%
where the time goes in v1:
time: 140 us; the launch traced here: 139 us
  blocking collectives  79.6 us (57%)
  starting transfers between devices  17.5 us (12%)
  matrix products  14.6 us (10%)
  local copies, waits for them, and re-layouts  13.2 us (9%)
  other arithmetic  7.03 us (5%)
  waiting for transfers between devices  6.51 us (5%)
    all_gather x1, blocking collectives, shards(): lax.all_gather(partial_gram, ('gx', 'gy'))  79.6 us
    ppermute x15, starting transfers between devices, partner(): return lax.ppermute(value, axis, pairs)  17.5 us
    dot_general x3, matrix products, shards(): jnp.einsum('rtij,rtjv->riv', tiles, operands, precision=lax.Precision.HIG...  14.3 us
    ppermute x15, waiting for transfers between devices, partner(): return lax.ppermute(value, axis, pairs)  6.51 us
    gather x3, local copies, waits for them, and re-layouts, shards(): operands = jnp.take(table, cols, axis=0)  5.09 us
    unnamed x38, local copies, waits for them, and re-layouts  4.88 us
  transfers between devices with their start and end apart: 15, of which 3 were waited for; matrix products, arithmetic and copies ran while one was open for 5% of the time, Pallas kernels for 0%

profile of v1, /device:TPU:0, one launch (start us, length us, event | category | flops | bytes accessed | tf_op | source)
XLA Modules:
  0.0 139.5 jit_solution(4179518517871306786)
XLA Ops:
  0.6 0.8 compare_and_fusion.1
  2.1 1.0 copy_bitcast_fusion.2
  3.7 3.0 %collective-permute-start.4 = (f32[2,128,64]{1,2,0:T(8,128)S(1)}, f32[2,128,64]{1,2,0:T(8,128)S(1)}, u32[]{:S(2)}, u32[]{:S(2)}) collective-permute-start(f32[2,128,64]{1,2,0:T(8,128)S(1)} %broadcast_select_fusion.2), channel_id=1, source_target_pairs={{0,16},{4,20},{8,24},{12,28},{16,0},{20,4},{24,8},{28,12},{1,17},{... | collective-permute-start | bytes 196616 | tf_op jit(solution)/shard_map/ppermute | solution.py:12
  6.7 1.5 %collective-permute-start.3 = (f32[2,128,64]{1,2,0:T(8,128)S(1)}, f32[2,128,64]{1,2,0:T(8,128)S(1)}, u32[]{:S(2)}, u32[]{:S(2)}) collective-permute-start(f32[2,128,64]{1,2,0:T(8,128)S(1)} %broadcast_select_fusion.2), channel_id=1, source_target_pairs={{0,8},{4,12},{8,0},{12,4},{16,24},{20,28},{24,16},{28,20},{1,9},{5... | collective-permute-start | bytes 196616 | tf_op jit(solution)/shard_map/ppermute | solution.py:12
  8.2 2.6 %collective-permute-start.1 = (f32[2,128,64]{1,2,0:T(8,128)S(1)}, f32[2,128,64]{1,2,0:T(8,128)S(1)}, u32[]{:S(2)}, u32[]{:S(2)}) collective-permute-start(f32[2,128,64]{1,2,0:T(8,128)S(1)} %broadcast_select_fusion.2), channel_id=1, source_target_pairs={{0,2},{1,3},{2,0},{3,1},{4,6},{5,7},{6,4},{7,5},{8,10},{9,11},{10,... | collective-permute-start | bytes 196616 | tf_op jit(solution)/shard_map/ppermute | solution.py:12
  10.8 1.6 %collective-permute-start = (f32[2,128,64]{1,2,0:T(8,128)S(1)}, f32[2,128,64]{1,2,0:T(8,128)}, u32[]{:S(2)}, u32[]{:S(2)}) collective-permute-start(f32[2,128,64]{1,2,0:T(8,128)S(1)} %broadcast_select_fusion.2), channel_id=1, source_target_pairs={{0,1},{1,0},{2,3},{3,2},{4,5},{5,4},{6,7},{7,6},{8,9},{9,8},{10,11... | collective-permute-start | bytes 196616 | tf_op jit(solution)/shard_map/ppermute | solution.py:12
  12.4 0.7 compare_and_fusion
  13.1 0.7 compare_select_fusion
  13.8 1.0 constant_dynamic-update-slice_fusion.5
  15.3 0.7 pad_clamp_fusion
  16.0 0.8 constant_dynamic-update-slice_fusion.4
  16.9 1.7 %gather_fusion.1 = f32[40,128,64]{1,2,0:T(8,128)} fusion(f32[18,128,64]{1,2,0:T(8,128)S(1)} %constant_dynamic-update-slice_fusion, s32[1024]{0:T(1024)S(1)} %pad_clamp_fusion), kind=kCustom, calls=%fused_computation.1.clone | custom fusion | bytes 2621600 | tf_op jit(solution)/shard_map/jit(_take)/gather | solution.py:38
  18.6 4.7 %fusion.6 = f32[8,8,8,128]{3,2,1,0:T(8,128)S(1)} fusion(f32[8,5,128,128]{3,2,1,0:T(8,128)S(1)} %copy-done, f32[8,5,128,64]{2,3,1,0:T(8,128)} %bitcast.86, pred[8,5]{1,0:T(8,128)(4,1)S(1)} %compare_and_fusion), kind=kOutput, calls=%fused_computation.12 | convolution fusion | flops 503644160 | bytes 4194344 | tf_op jit(solution)/shard_map/rtij,rtjv->riv/dot_general | solution.py:39
  23.4 0.7 copy-done.2
  25.8 0.8 collective-permute-start.6
  26.6 1.5 %collective-permute-start.5 = (f32[2,128,64]{1,2,0:T(8,128)S(1)}, f32[2,128,64]{1,2,0:T(8,128)S(1)}, u32[]{:S(2)}, u32[]{:S(2)}) collective-permute-start(f32[2,128,64]{1,2,0:T(8,128)S(1)} %broadcast_select_fusion.1), channel_id=1, source_target_pairs={{0,1},{1,0},{2,3},{3,2},{4,5},{5,4},{6,7},{7,6},{8,9},{9,8},{10,11... | collective-permute-start | bytes 196616 | tf_op jit(solution)/shard_map/ppermute | solution.py:12
  28.1 1.1 constant_dynamic-update-slice_fusion.11
  29.1 2.0 %collective-permute-done.5 = f32[2,128,64]{1,2,0:T(8,128)S(1)} collective-permute-done((f32[2,128,64]{1,2,0:T(8,128)S(1)}, f32[2,128,64]{1,2,0:T(8,128)S(1)}, u32[]{:S(2)}, u32[]{:S(2)}) %collective-permute-start.5) | collective-permute-done | bytes 65568 | tf_op jit(solution)/shard_map/ppermute | solution.py:12
  31.2 1.4 %collective-permute-done.6 = f32[2,128,64]{1,2,0:T(8,128)S(1)} collective-permute-done((f32[2,128,64]{1,2,0:T(8,128)S(1)}, f32[2,128,64]{1,2,0:T(8,128)S(1)}, u32[]{:S(2)}, u32[]{:S(2)}) %collective-permute-start.6) | collective-permute-done | bytes 65568 | tf_op jit(solution)/shard_map/ppermute | solution.py:12
  32.7 1.7 %gather_fusion.3 = f32[40,128,64]{1,2,0:T(8,128)} fusion(f32[18,128,64]{1,2,0:T(8,128)S(1)} %constant_dynamic-update-slice_fusion.6, s32[1024]{0:T(1024)S(1)} %pad_clamp_fusion), kind=kCustom, calls=%fused_computation.4.clone | custom fusion | bytes 2621600 | tf_op jit(solution)/shard_map/jit(_take)/gather | solution.py:38
  34.4 4.8 %fusion.9 = f32[8,8,8,128]{3,2,1,0:T(8,128)S(1)} fusion(f32[8,5,128,128]{3,2,1,0:T(8,128)S(1)} %copy-done, f32[8,5,128,64]{2,3,1,0:T(8,128)} %bitcast.87, pred[8,5]{1,0:T(8,128)(4,1)S(1)} %compare_and_fusion), kind=kOutput, calls=%fused_computation.13 | convolution fusion | flops 503644160 | bytes 4194344 | tf_op jit(solution)/shard_map/rtij,rtjv->riv/dot_general | solution.py:39
  39.9 0.7 copy-done.10
  41.2 1.5 %collective-permute-start.14 = (f32[2,128,64]{1,2,0:T(8,128)S(1)}, f32[2,128,64]{1,2,0:T(8,128)S(1)}, u32[]{:S(2)}, u32[]{:S(2)}) collective-permute-start(f32[2,128,64]{1,2,0:T(8,128)S(1)} %broadcast_select_fusion), channel_id=1, source_target_pairs={{0,16},{4,20},{8,24},{12,28},{16,0},{20,4},{24,8},{28,12},{1,17},{... | collective-permute-start | bytes 196616 | tf_op jit(solution)/shard_map/ppermute | solution.py:12
  42.8 1.5 %collective-permute-start.13 = (f32[2,128,64]{1,2,0:T(8,128)S(1)}, f32[2,128,64]{1,2,0:T(8,128)S(1)}, u32[]{:S(2)}, u32[]{:S(2)}) collective-permute-start(f32[2,128,64]{1,2,0:T(8,128)S(1)} %broadcast_select_fusion), channel_id=1, source_target_pairs={{0,8},{4,12},{8,0},{12,4},{16,24},{20,28},{24,16},{28,20},{1,9},{5... | collective-permute-start | bytes 196616 | tf_op jit(solution)/shard_map/ppermute | solution.py:12
  44.3 0.9 collective-permute-start.11
  45.2 1.7 %collective-permute-start.10 = (f32[2,128,64]{1,2,0:T(8,128)S(1)}, f32[2,128,64]{1,2,0:T(8,128)S(1)}, u32[]{:S(2)}, u32[]{:S(2)}) collective-permute-start(f32[2,128,64]{1,2,0:T(8,128)S(1)} %broadcast_select_fusion), channel_id=1, source_target_pairs={{0,1},{1,0},{2,3},{3,2},{4,5},{5,4},{6,7},{7,6},{8,9},{9,8},{10,11... | collective-permute-start | bytes 196616 | tf_op jit(solution)/shard_map/ppermute | solution.py:12
  46.8 1.0 constant_dynamic-update-slice_fusion.17
  47.8 3.0 %collective-permute-done.10 = f32[2,128,64]{1,2,0:T(8,128)S(1)} collective-permute-done((f32[2,128,64]{1,2,0:T(8,128)S(1)}, f32[2,128,64]{1,2,0:T(8,128)S(1)}, u32[]{:S(2)}, u32[]{:S(2)}) %collective-permute-start.10) | collective-permute-done | bytes 65568 | tf_op jit(solution)/shard_map/ppermute | solution.py:12
  50.9 1.7 %gather_fusion.5 = f32[40,128,64]{1,2,0:T(8,128)} fusion(f32[18,128,64]{1,2,0:T(8,128)S(1)} %constant_dynamic-update-slice_fusion.12, s32[1024]{0:T(1024)S(1)} %pad_clamp_fusion), kind=kCustom, calls=%fused_computation.5.clone | custom fusion | bytes 2621600 | tf_op jit(solution)/shard_map/jit(_take)/gather | solution.py:38
  52.6 4.8 %fusion.12 = f32[8,8,8,128]{3,2,1,0:T(8,128)S(1)} fusion(f32[8,5,128,128]{3,2,1,0:T(8,128)S(1)} %copy-done, f32[8,5,128,64]{2,3,1,0:T(8,128)} %bitcast.85, pred[8,5]{1,0:T(8,128)(4,1)S(1)} %compare_and_fusion), kind=kOutput, calls=%fused_computation.14 | convolution fusion | flops 503644160 | bytes 4194344 | tf_op jit(solution)/shard_map/rtij,rtjv->riv/dot_general | solution.py:39
  57.9 79.6 %all-gather = f32[2048,64]{1,0:T(8,128)} all-gather(f32[64,64]{1,0:T(8,128)S(1)} %fusion.32), channel_id=2, replica_groups=mesh['gx'=8,'gy'=4] {'gx','gy'}, dimensions={0}, use_global_device_ids=true | all-gather | bytes 540672 | tf_op jit(solution)/shard_map/all_gather | solution.py:48
  137.6 1.3 reduce_sum.9
  (68 shorter events, 6.2 us)
Async XLA Ops:
  0.6 18.0 %copy-start = (f32[8,5,128,128]{3,2,1,0:T(8,128)S(1)}, f32[8,5,128,128]{3,2,1,0:T(8,128)}, u32[]{:S(2)}) copy-start(f32[8,5,128,128]{3,2,1,0:T(8,128)} %param.9) | copy-start | bytes 7864324
  3.7 13.2 %collective-permute-start.4 = (f32[2,128,64]{1,2,0:T(8,128)S(1)}, f32[2,128,64]{1,2,0:T(8,128)S(1)}, u32[]{:S(2)}, u32[]{:S(2)}) collective-permute-start(f32[2,128,64]{1,2,0:T(8,128)S(1)} %broadcast_select_fusion.2), channel_id=1, source_target_pairs={{0,16},{4,20},{8,24},{12,28},{16,0},{20,4},{24,8},{28,12},{1,17},{... | collective-permute-start | bytes 196616 | tf_op jit(solution)/shard_map/ppermute | solution.py:12
  6.7 10.2 %collective-permute-start.3 = (f32[2,128,64]{1,2,0:T(8,128)S(1)}, f32[2,128,64]{1,2,0:T(8,128)S(1)}, u32[]{:S(2)}, u32[]{:S(2)}) collective-permute-start(f32[2,128,64]{1,2,0:T(8,128)S(1)} %broadcast_select_fusion.2), channel_id=1, source_target_pairs={{0,8},{4,12},{8,0},{12,4},{16,24},{20,28},{24,16},{28,20},{1,9},{5... | collective-permute-start | bytes 196616 | tf_op jit(solution)/shard_map/ppermute | solution.py:12
  8.2 8.6 %collective-permute-start.2 = (f32[2,128,64]{1,2,0:T(8,128)S(1)}, f32[2,128,64]{1,2,0:T(8,128)S(1)}, u32[]{:S(2)}, u32[]{:S(2)}) collective-permute-start(f32[2,128,64]{1,2,0:T(8,128)S(1)} %broadcast_select_fusion.2), channel_id=1, source_target_pairs={{0,4},{4,0},{8,12},{12,8},{16,20},{20,16},{24,28},{28,24},{1,5},{5... | collective-permute-start | bytes 196616 | tf_op jit(solution)/shard_map/ppermute | solution.py:12
  8.2 8.6 %collective-permute-start.1 = (f32[2,128,64]{1,2,0:T(8,128)S(1)}, f32[2,128,64]{1,2,0:T(8,128)S(1)}, u32[]{:S(2)}, u32[]{:S(2)}) collective-permute-start(f32[2,128,64]{1,2,0:T(8,128)S(1)} %broadcast_select_fusion.2), channel_id=1, source_target_pairs={{0,2},{1,3},{2,0},{3,1},{4,6},{5,7},{6,4},{7,5},{8,10},{9,11},{10,... | collective-permute-start | bytes 196616 | tf_op jit(solution)/shard_map/ppermute | solution.py:12
  10.8 5.2 %collective-permute-start = (f32[2,128,64]{1,2,0:T(8,128)S(1)}, f32[2,128,64]{1,2,0:T(8,128)}, u32[]{:S(2)}, u32[]{:S(2)}) collective-permute-start(f32[2,128,64]{1,2,0:T(8,128)S(1)} %broadcast_select_fusion.2), channel_id=1, source_target_pairs={{0,1},{1,0},{2,3},{3,2},{4,5},{5,4},{6,7},{7,6},{8,9},{9,8},{10,11... | collective-permute-start | bytes 196616 | tf_op jit(solution)/shard_map/ppermute | solution.py:12
  18.6 5.5 %copy-start.1 = (f32[1024,64]{0,1:T(8,128)S(1)}, f32[1024,64]{0,1:T(8,128)}, u32[]{:S(2)}) copy-start(f32[1024,64]{0,1:T(8,128)} %param.12) | copy-start | bytes 786436
  18.6 5.5 %copy-start.5 = (f32[1024,64]{0,1:T(8,128)S(1)}, f32[1024,64]{0,1:T(8,128)}, u32[]{:S(2)}) copy-start(f32[1024,64]{0,1:T(8,128)} %param.13) | copy-start | bytes 786436
  23.4 0.7 copy-start.2
  24.8 7.9 %collective-permute-start.9 = (f32[2,128,64]{1,2,0:T(8,128)S(1)}, f32[2,128,64]{1,2,0:T(8,128)S(1)}, u32[]{:S(2)}, u32[]{:S(2)}) collective-permute-start(f32[2,128,64]{1,2,0:T(8,128)S(1)} %broadcast_select_fusion.1), channel_id=1, source_target_pairs={{0,16},{4,20},{8,24},{12,28},{16,0},{20,4},{24,8},{28,12},{1,17},{... | collective-permute-start | bytes 196616 | tf_op jit(solution)/shard_map/ppermute | solution.py:12
  25.3 7.4 %collective-permute-start.8 = (f32[2,128,64]{1,2,0:T(8,128)S(1)}, f32[2,128,64]{1,2,0:T(8,128)S(1)}, u32[]{:S(2)}, u32[]{:S(2)}) collective-permute-start(f32[2,128,64]{1,2,0:T(8,128)S(1)} %broadcast_select_fusion.1), channel_id=1, source_target_pairs={{0,8},{4,12},{8,0},{12,4},{16,24},{20,28},{24,16},{28,20},{1,9},{5... | collective-permute-start | bytes 196616 | tf_op jit(solution)/shard_map/ppermute | solution.py:12
  25.8 6.8 %collective-permute-start.7 = (f32[2,128,64]{1,2,0:T(8,128)S(1)}, f32[2,128,64]{1,2,0:T(8,128)S(1)}, u32[]{:S(2)}, u32[]{:S(2)}) collective-permute-start(f32[2,128,64]{1,2,0:T(8,128)S(1)} %broadcast_select_fusion.1), channel_id=1, source_target_pairs={{0,4},{4,0},{8,12},{12,8},{16,20},{20,16},{24,28},{28,24},{1,5},{5... | collective-permute-start | bytes 196616 | tf_op jit(solution)/shard_map/ppermute | solution.py:12
  25.8 6.8 %collective-permute-start.6 = (f32[2,128,64]{1,2,0:T(8,128)S(1)}, f32[2,128,64]{1,2,0:T(8,128)S(1)}, u32[]{:S(2)}, u32[]{:S(2)}) collective-permute-start(f32[2,128,64]{1,2,0:T(8,128)S(1)} %broadcast_select_fusion.1), channel_id=1, source_target_pairs={{0,2},{1,3},{2,0},{3,1},{4,6},{5,7},{6,4},{7,5},{8,10},{9,11},{10,... | collective-permute-start | bytes 196616 | tf_op jit(solution)/shard_map/ppermute | solution.py:12
  26.6 4.6 %collective-permute-start.5 = (f32[2,128,64]{1,2,0:T(8,128)S(1)}, f32[2,128,64]{1,2,0:T(8,128)S(1)}, u32[]{:S(2)}, u32[]{:S(2)}) collective-permute-start(f32[2,128,64]{1,2,0:T(8,128)S(1)} %broadcast_select_fusion.1), channel_id=1, source_target_pairs={{0,1},{1,0},{2,3},{3,2},{4,5},{5,4},{6,7},{7,6},{8,9},{9,8},{10,11... | collective-permute-start | bytes 196616 | tf_op jit(solution)/shard_map/ppermute | solution.py:12
  34.4 4.8 %copy-start.3 = (f32[8,8,8,128]{3,2,1,0:T(8,128)S(1)}, f32[8,8,8,128]{3,2,1,0:T(8,128)}, u32[]{:S(2)}) copy-start(f32[8,8,8,128]{3,2,1,0:T(8,128)} %copy-done.2) | copy-start | bytes 786436
  34.4 4.8 %copy-start.6 = (f32[1024,64]{0,1:T(8,128)S(1)}, f32[1024,64]{0,1:T(8,128)}, u32[]{:S(2)}) copy-start(f32[1024,64]{0,1:T(8,128)} %param.13) | copy-start | bytes 786436
  39.2 0.7 copy-start.8
  39.9 0.7 copy-start.10
  41.2 9.6 %collective-permute-start.14 = (f32[2,128,64]{1,2,0:T(8,128)S(1)}, f32[2,128,64]{1,2,0:T(8,128)S(1)}, u32[]{:S(2)}, u32[]{:S(2)}) collective-permute-start(f32[2,128,64]{1,2,0:T(8,128)S(1)} %broadcast_select_fusion), channel_id=1, source_target_pairs={{0,16},{4,20},{8,24},{12,28},{16,0},{20,4},{24,8},{28,12},{1,17},{... | collective-permute-start | bytes 196616 | tf_op jit(solution)/shard_map/ppermute | solution.py:12
  42.8 8.1 %collective-permute-start.13 = (f32[2,128,64]{1,2,0:T(8,128)S(1)}, f32[2,128,64]{1,2,0:T(8,128)S(1)}, u32[]{:S(2)}, u32[]{:S(2)}) collective-permute-start(f32[2,128,64]{1,2,0:T(8,128)S(1)} %broadcast_select_fusion), channel_id=1, source_target_pairs={{0,8},{4,12},{8,0},{12,4},{16,24},{20,28},{24,16},{28,20},{1,9},{5... | collective-permute-start | bytes 196616 | tf_op jit(solution)/shard_map/ppermute | solution.py:12
  44.3 6.6 %collective-permute-start.12 = (f32[2,128,64]{1,2,0:T(8,128)S(1)}, f32[2,128,64]{1,2,0:T(8,128)S(1)}, u32[]{:S(2)}, u32[]{:S(2)}) collective-permute-start(f32[2,128,64]{1,2,0:T(8,128)S(1)} %broadcast_select_fusion), channel_id=1, source_target_pairs={{0,4},{4,0},{8,12},{12,8},{16,20},{20,16},{24,28},{28,24},{1,5},{5... | collective-permute-start | bytes 196616 | tf_op jit(solution)/shard_map/ppermute | solution.py:12
  44.3 6.5 %collective-permute-start.11 = (f32[2,128,64]{1,2,0:T(8,128)S(1)}, f32[2,128,64]{1,2,0:T(8,128)S(1)}, u32[]{:S(2)}, u32[]{:S(2)}) collective-permute-start(f32[2,128,64]{1,2,0:T(8,128)S(1)} %broadcast_select_fusion), channel_id=1, source_target_pairs={{0,2},{1,3},{2,0},{3,1},{4,6},{5,7},{6,4},{7,5},{8,10},{9,11},{10,... | collective-permute-start | bytes 196616 | tf_op jit(solution)/shard_map/ppermute | solution.py:12
  45.2 5.6 %collective-permute-start.10 = (f32[2,128,64]{1,2,0:T(8,128)S(1)}, f32[2,128,64]{1,2,0:T(8,128)S(1)}, u32[]{:S(2)}, u32[]{:S(2)}) collective-permute-start(f32[2,128,64]{1,2,0:T(8,128)S(1)} %broadcast_select_fusion), channel_id=1, source_target_pairs={{0,1},{1,0},{2,3},{3,2},{4,5},{5,4},{6,7},{7,6},{8,9},{9,8},{10,11... | collective-permute-start | bytes 196616 | tf_op jit(solution)/shard_map/ppermute | solution.py:12
  52.6 4.8 %copy-start.4 = (f32[8,8,8,128]{3,2,1,0:T(8,128)S(1)}, f32[8,8,8,128]{3,2,1,0:T(8,128)}, u32[]{:S(2)}) copy-start(f32[8,8,8,128]{3,2,1,0:T(8,128)} %copy-done.2) | copy-start | bytes 786436
  52.6 4.8 %copy-start.7 = (f32[1024,64]{0,1:T(8,128)S(1)}, f32[1024,64]{0,1:T(8,128)}, u32[]{:S(2)}) copy-start(f32[1024,64]{0,1:T(8,128)} %param.13) | copy-start | bytes 786436
  52.6 4.8 %copy-start.9 = (f32[8,8,8,128]{3,2,1,0:T(8,128)S(1)}, f32[8,8,8,128]{3,2,1,0:T(8,128)}, u32[]{:S(2)}) copy-start(f32[8,8,8,128]{3,2,1,0:T(8,128)} %copy-done.8) | copy-start | bytes 786436
  57.5 81.3 %copy-start.11 = (f32[1024,64]{0,1:T(8,128)}, f32[1024,64]{0,1:T(8,128)S(1)}, u32[]{:S(2)}) copy-start(f32[1024,64]{0,1:T(8,128)S(1)} %fusion.22) | copy-start | bytes 786436
